TPU v7x, 512 devices: a whole 4x4x16 slice. The times are simulated.
512 devices in a mesh: head: 8 (over x, core), ctx: 64 (over y, z).
Axes of the slice: x: 4, y: 4, z: 16, core: 2. Of those that a mesh axis runs over, the one named last changes fastest.
Arguments:
- queries: bfloat16 [8, 64, 1024, 128], P('head', 'ctx'), may hold values from -72 to 72
- keys: bfloat16 [8, 262144, 128], P('head', 'ctx'), may hold values from -24 to 24
- values: bfloat16 [8, 262144, 128], P('head', 'ctx'), may hold values from -6 to 6
- kept: int32 [8, 512], P('head'), may hold values from 0 to 262143, as said below
- roots: int32 [8], P('head'), may hold values from 0 to 63
Outputs:
- compact: float32 [8, 512, 128], P('head')
- fit_error: float32 [], replicated
Inputs may be any that keep to these rules, and one draw needn't show every extreme that they name: `kept`: per head: 512 distinct increasing positions; at most 32 of them lie within one context device's 4096 positions, and exactly 32 within at least one such device.
All inputs are finite; a program needn't handle non-finite values.
Results may differ from a plain program's by a relative error of at most 0.0003.
Values may be sent and summed in bfloat16 or wider, within the bound.
A program may use at most 64 MiB of HBM per device.

v0:
```python
import math
import jax
import jax.numpy as jnp
from jax import lax
from jax.sharding import PartitionSpec as P

HD = 128
KBLK = 1024
M = 512
ridge_share = 0.01


def spread(array, axis, root):
    mine = lax.axis_index(axis) == root
    return lax.psum(jnp.where(mine, array, jnp.zeros_like(array)), axis)


def merge_parts(first, second):
    first_max, first_sum, first_out = first
    second_max, second_sum, second_out = second
    joint = jnp.maximum(first_max, second_max)
    first_scale = jnp.exp(first_max - joint)
    second_scale = jnp.exp(second_max - joint)
    return (
        joint,
        first_sum * first_scale + second_sum * second_scale,
        first_out * first_scale[:, None] + second_out * second_scale[:, None],
    )


def block_partials(queries_ref, key_slab, value_slab, score_scale):
    blocks = key_slab.shape[0] // KBLK
    key_blocks = key_slab.reshape(blocks, KBLK, HD)
    value_blocks = value_slab.reshape(blocks, KBLK, HD)
    rows = queries_ref.shape[0]

    def visit(carry, pieces):
        key_block, value_block = pieces
        scores = (
            jnp.einsum("rd,kd->rk", queries_ref, key_block, preferred_element_type=jnp.float32)
            * score_scale
        )
        block_max = jnp.max(scores, axis=1)
        weights = jnp.exp(scores - block_max[:, None]).astype(jnp.bfloat16)
        block_sum = jnp.sum(weights.astype(jnp.float32), axis=1)
        block_out = jnp.dot(weights, value_block, preferred_element_type=jnp.float32)
        return (merge_parts(carry, (block_max, block_sum, block_out)), None)

    start = (
        jnp.full((rows,), -jnp.inf, jnp.float32),
        jnp.zeros((rows,), jnp.float32),
        jnp.zeros((rows, HD), jnp.float32),
    )
    return lax.scan(visit, start, (key_blocks, value_blocks))[0]


def compact_softmax(queries_ref, compact_keys, score_scale):
    scores = (
        jnp.einsum("rd,md->rm", queries_ref, compact_keys, preferred_element_type=jnp.float32)
        * score_scale
    )
    return jax.nn.softmax(scores, axis=1)


def inner_left(left, right):
    return lax.dot_general(
        left,
        right,
        (((0,), (0,)), ((), ())),
        precision=lax.Precision.HIGHEST,
        preferred_element_type=jnp.float32,
    )


def per_device(queries, keys, values, kept, roots):
    score_scale = 1.0 / math.sqrt(HD)
    queries_ref = spread(queries[0, 0], "ctx", roots[0])
    run_max, run_sum, run_out = block_partials(queries_ref, keys[0], values[0], score_scale)
    highest = lax.pmax(run_max, "ctx")
    rescale = jnp.exp(run_max - highest)
    run_sum, run_out = lax.psum((run_sum * rescale, run_out * rescale[:, None]), "ctx")
    target = run_out / run_sum[:, None]
    slab = keys.shape[1]
    shard = lax.axis_index("ctx")
    positions = kept[0]
    owner = positions // slab
    local_rows = positions - shard * slab
    mine = owner == shard
    picked = jnp.take(keys[0], jnp.clip(local_rows, 0, slab - 1), axis=0).astype(jnp.float32)
    picked = picked * mine.astype(jnp.float32)[:, None]
    compact_keys = lax.psum(picked, "ctx").astype(jnp.bfloat16)
    attend = compact_softmax(queries_ref, compact_keys, score_scale)
    gram = inner_left(attend, attend)
    cross = inner_left(attend, target)
    ridge = ridge_share * jnp.trace(gram) / M
    system = gram + ridge * jnp.eye(M, dtype=jnp.float32)
    factor_low = jnp.linalg.cholesky(system)
    halfway = lax.linalg.triangular_solve(factor_low, cross, left_side=True, lower=True)
    compact = lax.linalg.triangular_solve(
        factor_low, halfway, left_side=True, lower=True, transpose_a=True
    )
    target_square = jnp.sum(target * target)
    fitted_square = jnp.sum(
        compact
        * jnp.dot(
            gram, compact, precision=lax.Precision.HIGHEST, preferred_element_type=jnp.float32
        )
    )
    head_error = (target_square - 2.0 * jnp.sum(compact * cross) + fitted_square) / target_square
    fit_error = lax.psum(head_error, "head") / lax.axis_size("head")
    return (compact[None], fit_error)


def solution(mesh):
    placed = (
        P("head", "ctx", None, None),
        P("head", "ctx", None),
        P("head", "ctx", None),
        P("head", None),
        P("head"),
    )
    return jax.shard_map(
        per_device,
        mesh=mesh,
        in_specs=placed,
        out_specs=(P("head", None, None), P()),
        check_vma=False,
    )
```

profile of v0, /device:TPU:1, one launch (start us, length us, event | category | flops | bytes accessed | tf_op | source)
XLA Modules:
  0.0 929.7 jit_solution(15579256206267281522)
XLA Ops:
  12.7 260.3 %all-reduce.6.cloned.1.call-done = bf16[1024,128]{1,0:T(8,128)(2,1)} async-done(((bf16[1024,128]{1,0:T(8,128)(2,1)}), bf16[1024,128]{1,0:T(8,128)(2,1)}) %all-reduce.6.cloned.1.call-update) | async-done | bytes 262160 | tf_op jit(solution)/shard_map/psum | solution.py:15
  273.0 31.4 %while.17 = (s32[]{:T(128)}, f32[1024]{0:T(1024)S(1)}, f32[1024]{0:T(1024)S(1)}, f32[1024,128]{1,0:T(8,128)S(1)}, bf16[4,1024,128]{2,1,0:T(8,128)(2,1)}, /*index...) while((s32[]{:T(128)}, f32[1024]{0:T(1024)S(1)}, ...), condition=%wide.region_16.17_spmd.clone, body=%wide.region_13.16_spmd.clone.sunk | while | flops 547887104 | bytes 31252628 | solution.py:54
  277.4 3.4 fusion.100
  285.3 3.4 fusion.100
  293.1 3.4 fusion.100
  301.0 3.4 fusion.100
  304.4 113.1 %pmax.7 = f32[1024]{0:T(1024)S(1)} all-reduce(f32[1024]{0:T(1024)S(1)} %get-tuple-element.42), channel_id=1, replica_groups=mesh['head'=8,'ctx'=64] {'ctx'}, use_global_device_ids=true, to_apply=%region_17.18 | all-reduce | flops 1024 | bytes 8192 | tf_op jit(solution)/shard_map/pmax | solution.py:79
  418.5 222.3 %all-reduce.9 = (bf16[512,128]{1,0:T(8,128)(2,1)S(1)}, f32[1024]{0:T(1024)S(1)}) all-reduce(f32[512,128]{1,0:T(8,128)S(1)} %convert_multiply_fusion, f32[1024]{0:T(1024)S(1)} %get-tuple-element.104), channel_id=1, replica_groups=mesh['head'=8,'ctx'=64] {'ctx'}, use_global_device_ids=true, to_apply=%region_1.2 | all-reduce | flops 66560 | bytes 401408 | tf_op jit(solution)/shard_map/psum | solution.py:91
  642.6 4.7 select_reduce_fusion
  651.8 11.7 %cholesky.103 = f32[128,128]{1,0:T(8,128)S(1)} custom-call(f32[128,128]{1,0:T(8,128)S(1)} %cholesky.263), custom_call_target="Cholesky" | custom-call | tf_op jit(solution)/shard_map/jit(cholesky)/cholesky | solution.py:97
  664.7 9.8 %custom-call.32 = f32[1,128,128]{1,2,0:T(8,128)S(1)} custom-call(f32[1,128,128]{2,1,0:T(8,128)S(1)} %get-tuple-element.121), custom_call_target="InvertDiagBlocksLowerTriangular" | custom-call | tf_op jit(solution)/shard_map/jit(cholesky)/cholesky | solution.py:97
  677.7 12.2 %cholesky.215 = f32[128,128]{1,0:T(8,128)S(1)} custom-call(f32[128,128]{1,0:T(8,128)S(1)} %cholesky.267), custom_call_target="Cholesky" | custom-call | tf_op jit(solution)/shard_map/jit(cholesky)/cholesky | solution.py:97
  690.6 9.8 %custom-call.33 = f32[1,128,128]{1,2,0:T(8,128)S(1)} custom-call(f32[1,128,128]{2,1,0:T(8,128)S(1)} %get-tuple-element.118), custom_call_target="InvertDiagBlocksLowerTriangular" | custom-call | tf_op jit(solution)/shard_map/jit(cholesky)/cholesky | solution.py:97
  702.8 11.7 %cholesky.236 = f32[128,128]{1,0:T(8,128)S(1)} custom-call(f32[128,128]{1,0:T(8,128)S(1)} %cholesky.272), custom_call_target="Cholesky" | custom-call | tf_op jit(solution)/shard_map/jit(cholesky)/cholesky | solution.py:97
  715.1 9.8 %custom-call.34 = f32[1,128,128]{1,2,0:T(8,128)S(1)} custom-call(f32[1,128,128]{2,1,0:T(8,128)S(1)} %get-tuple-element.115), custom_call_target="InvertDiagBlocksLowerTriangular" | custom-call | tf_op jit(solution)/shard_map/jit(cholesky)/cholesky | solution.py:97
  727.4 11.7 %cholesky.253 = f32[128,128]{1,0:T(8,128)S(1)} custom-call(f32[128,128]{1,0:T(8,128)S(1)} %convolution_subtract_fusion.8), custom_call_target="Cholesky" | custom-call | tf_op jit(solution)/shard_map/jit(cholesky)/cholesky | solution.py:97
  746.6 14.4 %while.16 = (s32[]{:T(128)}, f32[512,512]{1,0:T(8,128)}, s32[4,2]{0,1:T(2,128)S(1)}, f32[4,128,128]{2,1,0:T(8,128)}, s32[]{:T(128)}) while((s32[]{:T(128)}, f32[512,512]{1,0:T(8,128)}, s32[4,2]{0,1:T(2,128)S(1)}, f32[4,128,128]{2,1,0:T(8,128)}, s32[]{:T(128)}) %tuple.64), condition=%wide.while_cond, body=%wide.while_body.sunk | while | flops 2 | bytes 132205 | solution.py:99
  747.3 3.0 bitcast_dynamic-update-slice_fusion.2
  750.9 3.0 bitcast_dynamic-update-slice_fusion.2
  754.6 3.0 bitcast_dynamic-update-slice_fusion.2
  758.2 2.9 bitcast_dynamic-update-slice_fusion.2
  761.1 40.3 %custom-call.35 = f32[4,128,128]{1,2,0:T(8,128)S(1)} custom-call(f32[4,128,128]{2,1,0:T(8,128)} %get-tuple-element.51), custom_call_target="InvertDiagBlocksLowerTriangular" | custom-call | tf_op jit(solution)/shard_map/triangular_solve | solution.py:99
  801.4 3.2 fusion.15
  815.1 105.7 %psum.39 = f32[]{:T(128)} all-reduce(f32[]{:T(128)S(6)} %div.56), channel_id=1, replica_groups=mesh['head'=8,'ctx'=64] {'head'}, use_global_device_ids=true, to_apply=%region_23.24 | all-reduce | flops 1 | bytes 8 | tf_op jit(solution)/shard_map/psum | solution.py:110
  (92 shorter events, 55.0 us)
Async XLA Ops:
  7.2 265.8 %all-reduce.6.cloned.1.call-start = ((), (), s32[]{:S(2)}) async-start(), calls=%async_computation | async-start | bytes 524288 | tf_op jit(solution)/shard_map/psum | solution.py:15
  8.6 792.8 %all-reduce.8.cloned.1.call-start = ((), (), s32[]{:S(2)}) async-start(), calls=%async_computation.1 | async-start | bytes 1048576 | tf_op jit(solution)/shard_map/psum | solution.py:81
  274.7 1.9 copy-start
  282.6 1.9 copy-start
  290.4 1.9 copy-start
  298.3 1.9 copy-start
  650.7 1.0 copy-start.2
  801.4 3.5 copy-start.1
  806.3 6.0 copy-start.3
Sparse Core Ops, SparseCore 0:
  12.0 260.9 all-reduce.5
  418.6 285.3 all-reduce.7
where the time goes:
time: 934 us; the launch traced here: 930 us
  blocking collectives  441 us (47%)
  waiting for transfers between devices  260 us (28%)
  other arithmetic  134 us (14%)
  matrix products  43.4 us (5%)
  local copies, waits for them, and re-layouts  28 us (3%)
  between operations  22.9 us (2%)
    psum x1, waiting for transfers between devices, spread(): return lax.psum(jnp.where(mine, array, jnp.zeros_like(array)), axis)  260 us
    psum x1, blocking collectives, per_device(): compact_keys = lax.psum(picked, 'ctx').astype(jnp.bfloat16)  222 us
    pmax x1, blocking collectives, per_device(): highest = lax.pmax(run_max, 'ctx')  113 us
    psum x1, blocking collectives, per_device(): fit_error = lax.psum(head_error, 'head') / lax.axis_size('head')  106 us
    another operation x14, other arithmetic, per_device(): factor_low = jnp.linalg.cholesky(system)  80.8 us
    another operation x3, other arithmetic, per_device(): lax.linalg.triangular_solve(factor_low, halfway, left_side=True, lower=Tr...  42.7 us
  transfers between devices with their start and end apart: 2, of which 1 were waited for; matrix products, arithmetic and copies ran while one was open for 17% of the time, Pallas kernels for 0%

commit v1 on v0

--- a/solution.py
+++ b/solution.py
@@ -12,7 +12,10 @@
 
 def spread(array, axis, root):
     mine = lax.axis_index(axis) == root
-    return lax.psum(jnp.where(mine, array, jnp.zeros_like(array)), axis)
+    spread_slabs = lambda local_block, group_axis: jnp.sum(
+        lax.all_gather(local_block, group_axis), axis=0
+    )
+    return spread_slabs(jnp.where(mine, array, jnp.zeros_like(array)), axis)
 
 
 def merge_parts(first, second):

time: 934 us -> 1060 us (1.13)
  waiting for transfers between devices: 260 us -> 473 us
  blocking collectives: 441 us -> 358 us
    psum x1, waiting for transfers between devices: 0.02 us -> 277 us  [per_device(): lax.psum((run_sum * rescale, run_out * rescale[:, None]), 'ctx')]
    psum x1 -> x0, waiting for transfers between devices: 260 us -> none  [spread(): return lax.psum(jnp.where(mine, array, jnp.zeros_like(array)), axis)]
    all_gather x0 -> x1, waiting for transfers between devices: none -> 196 us  [spread(): lax.all_gather(local_block, group_axis)]
    psum x1, blocking collectives: 106 us -> 23 us  [per_device(): fit_error = lax.psum(head_error, 'head') / lax.axis_size('head')]
  transfers between devices with their start and end apart: 2 -> 2, of which waited for: 1 -> 2; matrix products, arithmetic and copies ran while one was open for 17% -> 5% of each run, Pallas kernels for 0% -> 0%
where the time goes in v1:
time: 1060 us; the launch traced here: 1050 us
  waiting for transfers between devices  473 us (45%)
  blocking collectives  358 us (34%)
  other arithmetic  137 us (13%)
  matrix products  40.5 us (4%)
  local copies, waits for them, and re-layouts  22.9 us (2%)
  between operations  22.9 us (2%)
    psum x1, waiting for transfers between devices, per_device(): lax.psum((run_sum * rescale, run_out * rescale[:, None]), 'ctx')  277 us
    psum x1, blocking collectives, per_device(): compact_keys = lax.psum(picked, 'ctx').astype(jnp.bfloat16)  223 us
    all_gather x1, waiting for transfers between devices, spread(): lax.all_gather(local_block, group_axis)  196 us
    pmax x1, blocking collectives, per_device(): highest = lax.pmax(run_max, 'ctx')  112 us
    another operation x14, other arithmetic, per_device(): factor_low = jnp.linalg.cholesky(system)  78.9 us
    another operation x3, other arithmetic, per_device(): lax.linalg.triangular_solve(factor_low, halfway, left_side=True, lower=Tr...  40.6 us
    psum x1, blocking collectives, per_device(): fit_error = lax.psum(head_error, 'head') / lax.axis_size('head')  23 us
  transfers between devices with their start and end apart: 2, of which 2 were waited for; matrix products, arithmetic and copies ran while one was open for 5% of the time, Pallas kernels for 0%

profile of v1, /device:TPU:1, one launch (start us, length us, event | category | flops | bytes accessed | tf_op | source)
XLA Modules:
  0.0 1054.9 jit_solution(16757393772805951007)
XLA Ops:
  9.4 2.4 gather_fusion
  12.7 196.2 %all-gather.3.cloned.1.call-done = bf16[64,1,1024,128]{3,2,1,0:T(8,128)(2,1)} async-done(((bf16[1,1,1024,128]{3,2,1,0:T(8,128)(2,1)}), bf16[64,1,1024,128]{3,2,1,0:T(8,128)(2,1)}) %all-gather.3.cloned.1.call-update) | async-done | bytes 16777232 | tf_op jit(solution)/shard_map/all_gather | solution.py:16
  209.0 8.8 reduce_sum.67
  217.8 31.1 %while.17 = (s32[]{:T(128)}, f32[1024]{0:T(1024)S(1)}, f32[1024]{0:T(1024)S(1)}, f32[1024,128]{1,0:T(8,128)S(1)}, bf16[4,1024,128]{2,1,0:T(8,128)(2,1)}, /*index...) while((s32[]{:T(128)}, f32[1024]{0:T(1024)S(1)}, ...), condition=%wide.region_16.17_spmd.clone, body=%wide.region_13.16_spmd.clone.sunk | while | flops 547887104 | bytes 31253636 | solution.py:57
  222.1 3.4 fusion.100
  229.9 3.4 fusion.100
  237.7 3.4 fusion.100
  245.4 3.4 fusion.100
  248.8 111.9 %pmax.7 = f32[1024]{0:T(1024)S(1)} all-reduce(f32[1024]{0:T(1024)S(1)} %get-tuple-element.42), channel_id=1, replica_groups=mesh['head'=8,'ctx'=64] {'ctx'}, use_global_device_ids=true, to_apply=%region_17.18 | all-reduce | flops 1024 | bytes 8192 | tf_op jit(solution)/shard_map/pmax | solution.py:82
  360.7 222.8 %all-reduce.6 = (bf16[512,128]{1,0:T(8,128)(2,1)S(1)}, f32[1024]{0:T(1024)S(1)}) all-reduce(f32[512,128]{1,0:T(8,128)S(1)} %convert_multiply_fusion, f32[1024]{0:T(1024)S(1)} %get-tuple-element.104), channel_id=1, replica_groups=mesh['head'=8,'ctx'=64] {'ctx'}, use_global_device_ids=true, to_apply=%region_1.2 | all-reduce | flops 66560 | bytes 401408 | tf_op jit(solution)/shard_map/psum | solution.py:94
  584.3 4.7 select_reduce_fusion
  591.3 11.7 %cholesky.103 = f32[128,128]{1,0:T(8,128)S(1)} custom-call(f32[128,128]{1,0:T(8,128)S(1)} %cholesky.263), custom_call_target="Cholesky" | custom-call | tf_op jit(solution)/shard_map/jit(cholesky)/cholesky | solution.py:100
  603.2 9.8 custom-call.32
  615.5 12.2 %cholesky.215 = f32[128,128]{1,0:T(8,128)S(1)} custom-call(f32[128,128]{1,0:T(8,128)S(1)} %cholesky.267), custom_call_target="Cholesky" | custom-call | tf_op jit(solution)/shard_map/jit(cholesky)/cholesky | solution.py:100
  627.8 9.8 custom-call.33
  639.1 11.7 %cholesky.236 = f32[128,128]{1,0:T(8,128)S(1)} custom-call(f32[128,128]{1,0:T(8,128)S(1)} %cholesky.272), custom_call_target="Cholesky" | custom-call | tf_op jit(solution)/shard_map/jit(cholesky)/cholesky | solution.py:100
  651.5 9.8 custom-call.34
  663.0 11.7 %cholesky.253 = f32[128,128]{1,0:T(8,128)S(1)} custom-call(f32[128,128]{1,0:T(8,128)S(1)} %convolution_subtract_fusion.8), custom_call_target="Cholesky" | custom-call | tf_op jit(solution)/shard_map/jit(cholesky)/cholesky | solution.py:100
  680.7 11.4 %while.16 = (s32[]{:T(128)}, f32[512,512]{1,0:T(8,128)}, s32[4,2]{0,1:T(2,128)S(1)}, f32[4,128,128]{2,1,0:T(8,128)S(1)}, s32[]{:T(128)}) while((s32[]{:T(128)}, f32[512,512]{1,0:T(8,128)}, s32[4,2]{0,1:T(2,128)S(1)}, f32[4,128,128]{2,1,0:T(8,128)S(1)}, s32[]{:T(128)}) %tuple.64), condition=%wide.while_cond, body=%wide.while_body.sunk | while | flops 2 | bytes 131181 | solution.py:102
  681.3 2.3 bitcast_dynamic-update-slice_fusion.2
  692.1 39.5 %custom-call.35 = f32[4,128,128]{1,2,0:T(8,128)S(1)} custom-call(f32[4,128,128]{2,1,0:T(8,128)S(1)} %get-tuple-element.51), custom_call_target="InvertDiagBlocksLowerTriangular" | custom-call | tf_op jit(solution)/shard_map/triangular_solve | solution.py:102
  731.7 277.1 %all-reduce.5.cloned.1.call-done = f32[1024,128]{1,0:T(8,128)} async-done(((f32[1024,128]{1,0:T(8,128)}), f32[1024,128]{1,0:T(8,128)}) %all-reduce.5.cloned.1.call-update) | async-done | bytes 524304 | tf_op jit(solution)/shard_map/psum | solution.py:84
  1008.8 3.8 fusion.15
  1023.1 23.0 %psum.31 = f32[]{:T(128)} all-reduce(f32[]{:T(128)S(6)} %div.56), channel_id=1, replica_groups=mesh['head'=8,'ctx'=64] {'head'}, use_global_device_ids=true, to_apply=%region_23.24 | all-reduce | flops 1 | bytes 8 | tf_op jit(solution)/shard_map/psum | solution.py:113
  (95 shorter events, 49.0 us)
Async XLA Ops:
  7.2 201.8 %all-gather.3.cloned.1.call-start = ((), (), s32[]{:S(2)}) async-start(), calls=%async_computation.1 | async-start | bytes 17039360 | tf_op jit(solution)/shard_map/all_gather | solution.py:16
  8.6 1000.2 %all-reduce.5.cloned.1.call-start = ((), (), s32[]{:S(2)}) async-start(), calls=%async_computation | async-start | bytes 1048576 | tf_op jit(solution)/shard_map/psum | solution.py:84
  219.4 1.9 copy-start
  227.2 1.9 copy-start
  235.0 1.9 copy-start
  242.8 1.9 copy-start
  583.9 5.1 copy-start.1
  590.3 1.0 copy-start.3
  1008.8 4.1 copy-start.2
  1014.3 6.0 copy-start.4
Sparse Core Ops, SparseCore 0:
  11.5 197.4 all-gather.2
  676.5 332.2 all-reduce.4
